TPU v7x, 32 devices: a whole 2x2x4 slice. The times are simulated.
32 devices in a mesh: blk: 4 (over y, x), strata: 8 (over z, core).
Axes of the slice: x: 2, y: 2, z: 4, core: 2. Of those that a mesh axis runs over, the one named last changes fastest.
Arguments:
- user_factors: bfloat16 [4096, 256], P('blk'), may hold values from -1.5 to 1.5
- item_factors: bfloat16 [8192, 256], P(('blk', 'strata')), may hold values from -1.5 to 1.5
- ratings: bfloat16 [4, 4, 8, 8, 128, 128], P('blk', None, 'strata'), may hold values from -6 to 6
- tile_user: int32 [4, 4, 8, 8], P('blk', None, 'strata'), may hold values from 0 to 7
- tile_item: int32 [4, 4, 8, 8], P('blk', None, 'strata'), may hold values from 0 to 1
- tile_count: int32 [4, 4, 8], P('blk', None, 'strata'), may hold values from 1 to 8, 40 in all within a row
Outputs:
- user_grad: float32 [4096, 256], P('blk')
- item_grad: float32 [8192, 256], P(('blk', 'strata'))
Inputs may be any that keep to these rules, and one draw needn't show every extreme that they name: `tile_count`: for each user block and panel index, the counts over the strata are uneven and one of them equals 8.
All inputs are finite; a program needn't handle non-finite values.
Results may differ from a plain program's by a relative error of at most 0.0012.
Values may be sent and summed in bfloat16 or wider, within the bound.
A program may use at most 64 MiB of HBM per device.

v0:
```python
import jax
import jax.numpy as jnp
from jax import lax
from jax.sharding import PartitionSpec as P


def tile_terms(user_tiles, panel_tiles, rating_tiles, rows, cols, count):
    slots = rating_tiles.shape[0]
    tile = rating_tiles.shape[-1]
    picked_users = jnp.take(user_tiles, rows, axis=0)
    picked_items = jnp.take(panel_tiles, cols, axis=0)
    predicted = jnp.einsum(
        "kar,kbr->kab", picked_users, picked_items, preferred_element_type=jnp.float32
    )
    live = (jnp.arange(slots) < count).astype(jnp.float32)
    residue = ((predicted - rating_tiles.astype(jnp.float32)) * live[:, None, None]).astype(
        jnp.bfloat16
    )
    user_part = (
        jnp.einsum("kab,kbr->kar", residue, picked_items, preferred_element_type=jnp.float32) / tile
    )
    item_part = (
        jnp.einsum("kab,kar->kbr", residue, picked_users, preferred_element_type=jnp.float32) / tile
    )
    user_hot = (rows[:, None] == jnp.arange(user_tiles.shape[0])[None, :]).astype(jnp.float32)
    item_hot = (cols[:, None] == jnp.arange(panel_tiles.shape[0])[None, :]).astype(jnp.float32)
    user_sum = jnp.einsum("ku,kar->uar", user_hot, user_part, precision=lax.Precision.HIGHEST)
    item_sum = jnp.einsum("kp,kbr->pbr", item_hot, item_part, precision=lax.Precision.HIGHEST)
    return (user_sum, item_sum)


def settle_early(user_total, early):
    return (user_total, early)


def body(user_factors, item_factors, ratings, tile_user, tile_item, tile_count):
    steps = lax.axis_size("blk")
    tile = ratings.shape[-1]
    rank = user_factors.shape[1]
    panel_rows = item_factors.shape[0]
    user_tiles = user_factors.reshape(-1, tile, rank)
    rating_sets = ratings[0, :, 0]
    row_sets = tile_user[0, :, 0]
    col_sets = tile_item[0, :, 0]
    count_sets = tile_count[0, :, 0]
    user_total = jnp.zeros(user_tiles.shape, jnp.float32)
    early = None
    gathered = lax.all_gather(item_factors, "blk", axis=0, tiled=True)
    pieces = []
    for source in range(steps):
        panel = gathered[source * panel_rows : (source + 1) * panel_rows]
        rating_tiles = lax.dynamic_index_in_dim(rating_sets, source, 0, keepdims=False)
        rows = lax.dynamic_index_in_dim(row_sets, source, 0, keepdims=False)
        cols = lax.dynamic_index_in_dim(col_sets, source, 0, keepdims=False)
        count = lax.dynamic_index_in_dim(count_sets, source, 0, keepdims=False)
        user_part, item_part = tile_terms(
            user_tiles, panel.reshape(-1, tile, rank), rating_tiles, rows, cols, count
        )
        user_total = user_total + user_part
        pieces.append(item_part.reshape(panel_rows, rank))
        user_total, early = settle_early(user_total, early)
    item_grad = lax.psum_scatter(
        jnp.concatenate(pieces, axis=0), "blk", scatter_dimension=0, tiled=True
    )
    user_grad = lax.psum(user_total, "strata")
    return (user_grad.reshape(-1, rank), item_grad)


def solution(mesh):
    in_specs = (
        P("blk", None),
        P(("blk", "strata"), None),
        P("blk", None, "strata", None, None, None),
        P("blk", None, "strata", None),
        P("blk", None, "strata", None),
        P("blk", None, "strata"),
    )
    out_specs = (P("blk", None), P(("blk", "strata"), None))
    return jax.shard_map(body, mesh=mesh, in_specs=in_specs, out_specs=out_specs, check_vma=False)
```

profile of v0, /device:TPU:0, one launch (start us, length us, event | category | flops | bytes accessed | tf_op | source)
XLA Modules:
  0.0 119.4 jit_solution(5555860137044684791)
XLA Ops:
  8.1 0.8 compare_and_fusion.1
  8.9 0.7 copy-done.17
  9.5 11.8 %all_gather.3 = bf16[1024,256]{1,0:T(8,128)(2,1)S(1)} all-gather(bf16[256,256]{1,0:T(8,128)(2,1)} %param.11), channel_id=1, replica_groups=mesh['blk'=4,'strata'=8] {'blk'}, dimensions={0}, use_global_device_ids=true | all-gather | bytes 655360 | tf_op jit(solution)/shard_map/all_gather | solution.py:48
  21.4 0.6 copy-done.18
  22.0 0.6 fusion.78
  22.7 0.6 compare_convert_fusion.1
  23.3 1.4 %gather_fusion.4 = bf16[8,128,256]{2,1,0:T(8,128)(2,1)} fusion(bf16[8,128,256]{2,1,0:T(8,128)(2,1)S(1)} %bitcast.100, s32[1024]{0:T(1024)S(1)} %get-tuple-element.49), kind=kCustom, calls=%fused_computation.3.clone | custom fusion | bytes 1048608 | tf_op jit(solution)/shard_map/jit(_take)/gather | solution.py:10
  24.7 0.6 gather_fusion.6
  25.3 0.7 compare_convert_fusion
  25.9 0.6 gather_fusion.2
  26.5 0.7 compare_convert_fusion.2
  27.2 0.6 gather_fusion
  27.8 0.6 compare_convert_fusion.3
  28.5 1.4 %gather_fusion.1 = bf16[8,128,256]{2,1,0:T(8,128)(2,1)} fusion(bf16[2,128,256]{2,1,0:T(8,128)(2,1)S(1)} %bitcast.106, s32[1024]{0:T(1024)S(1)} %get-tuple-element.55), kind=kCustom, calls=%fused_computation.1.clone | custom fusion | bytes 1048608 | tf_op jit(solution)/shard_map/jit(_take)/gather | solution.py:11
  29.9 1.5 %fusion.4 = bf16[8,128,128]{2,1,0:T(8,128)(2,1)S(1)} fusion(f32[8]{0:T(128)S(1)} %compare_convert_fusion.3, bf16[1,4,1,8,128,128]{5,4,3,2,1,0:T(8,128)(2,1)} %param.12, bf16[8,128,256]{2,1,0:T(8,128)(2,1)S(1)} %gather_fusion, pred[8]{0:T(512)(128)(4,1)S(1)} %get-tuple-element.42, bf16[8,128,256]{2,1,0:T(8,128)(2,1)} %gather_fusion.1, ...), kind=kOutput, calls=%fused_computation.19 | convolution fusion | flops 68157440 | bytes 1572912 | tf_op jit(solution)/shard_map/kar,kbr->kab/dot_general | solution.py:12
  31.4 1.5 %fusion.22 = f32[8,128,256]{2,1,0:T(8,128)S(1)} fusion(bf16[8,128,128]{2,1,0:T(8,128)(2,1)S(1)} %fusion.4, bf16[8,128,256]{2,1,0:T(8,128)(2,1)} %gather_fusion.1, pred[8]{0:T(512)(128)(4,1)S(1)} %get-tuple-element.36), kind=kOutput, calls=%fused_computation.54 | convolution fusion | flops 67371008 | bytes 1835016 | tf_op jit(solution)/shard_map/kab,kbr->kar/dot_general | solution.py:20
  32.9 1.4 %gather_fusion.3 = bf16[8,128,256]{2,1,0:T(8,128)(2,1)} fusion(bf16[2,128,256]{2,1,0:T(8,128)(2,1)S(1)} %bitcast.105, s32[1024]{0:T(1024)S(1)} %get-tuple-element.54), kind=kCustom, calls=%fused_computation.5.clone | custom fusion | bytes 1048608 | tf_op jit(solution)/shard_map/jit(_take)/gather | solution.py:11
  34.3 1.6 %fusion.5 = bf16[8,128,128]{2,1,0:T(8,128)(2,1)S(1)} fusion(f32[8]{0:T(128)S(1)} %compare_convert_fusion.2, bf16[1,4,1,8,128,128]{5,4,3,2,1,0:T(8,128)(2,1)} %param.12, bf16[8,128,256]{2,1,0:T(8,128)(2,1)S(1)} %gather_fusion.2, pred[8]{0:T(512)(128)(4,1)S(1)} %get-tuple-element.40, bf16[8,128,256]{2,1,0:T(8,128)(2,1)} %gather_fusion.3, ...), kind=kOutput, calls=%fused_computation.20 | convolution fusion | flops 68157440 | bytes 1572912 | tf_op jit(solution)/shard_map/kar,kbr->kab/dot_general | solution.py:12
  35.8 0.4 fusion.24
  36.2 0.3 copy-done.12
  36.5 1.4 %gather_fusion.5 = bf16[8,128,256]{2,1,0:T(8,128)(2,1)} fusion(bf16[2,128,256]{2,1,0:T(8,128)(2,1)S(1)} %bitcast.104, s32[1024]{0:T(1024)S(1)} %get-tuple-element.53), kind=kCustom, calls=%fused_computation.6.clone | custom fusion | bytes 1048608 | tf_op jit(solution)/shard_map/jit(_take)/gather | solution.py:11
  37.9 1.7 %fusion.6 = bf16[8,128,128]{2,1,0:T(8,128)(2,1)S(1)} fusion(f32[8]{0:T(128)S(1)} %compare_convert_fusion.1, bf16[1,4,1,8,128,128]{5,4,3,2,1,0:T(8,128)(2,1)} %param.12, bf16[8,128,256]{2,1,0:T(8,128)(2,1)} %gather_fusion.4, pred[8]{0:T(512)(128)(4,1)S(1)} %get-tuple-element.38, bf16[8,128,256]{2,1,0:T(8,128)(2,1)} %gather_fusion.5, ...), kind=kOutput, calls=%fused_computation.21 | convolution fusion | flops 68157440 | bytes 1572912 | tf_op jit(solution)/shard_map/kar,kbr->kab/dot_general | solution.py:12
  39.7 1.3 %fusion.26 = f32[8,128,256]{2,1,0:T(8,128)} fusion(bf16[8,128,128]{2,1,0:T(8,128)(2,1)S(1)} %fusion.6, bf16[8,128,256]{2,1,0:T(8,128)(2,1)S(1)} %copy-done.9, pred[8]{0:T(512)(128)(4,1)S(1)} %get-tuple-element.32), kind=kOutput, calls=%fused_computation.58 | convolution fusion | flops 67371008 | bytes 1835016 | tf_op jit(solution)/shard_map/kab,kbr->kar/dot_general | solution.py:20
  41.0 1.4 %gather_fusion.7 = bf16[8,128,256]{2,1,0:T(8,128)(2,1)} fusion(bf16[2,128,256]{2,1,0:T(8,128)(2,1)S(1)} %bitcast.103, s32[1024]{0:T(1024)S(1)} %get-tuple-element.52), kind=kCustom, calls=%fused_computation.7.clone | custom fusion | bytes 1048608 | tf_op jit(solution)/shard_map/jit(_take)/gather | solution.py:11
  42.4 1.5 %fusion.7 = bf16[8,128,128]{2,1,0:T(8,128)(2,1)S(1)} fusion(f32[8]{0:T(128)S(1)} %compare_convert_fusion, bf16[1,4,1,8,128,128]{5,4,3,2,1,0:T(8,128)(2,1)} %param.12, bf16[8,128,256]{2,1,0:T(8,128)(2,1)S(1)} %gather_fusion.6, pred[8]{0:T(512)(128)(4,1)S(1)} %get-tuple-element.6, bf16[8,128,256]{2,1,0:T(8,128)(2,1)} %gather_fusion.7, ...), kind=kOutput, calls=%fused_computation.22 | convolution fusion | flops 68157440 | bytes 1572912 | tf_op jit(solution)/shard_map/kar,kbr->kab/dot_general | solution.py:12
  43.9 0.4 fusion.28
  44.3 1.2 fusion.12
  45.5 1.2 convolution_add_fusion.2
  46.7 1.2 convolution_add_fusion.1
  47.9 1.2 convolution_add_fusion
  49.1 1.3 %copy.8 = f32[8,128,256]{2,1,0:T(8,128)} copy(f32[8,128,256]{2,0,1:T(8,128)S(1)} %convolution_add_fusion) | data formatting | bytes 2097152 | tf_op jit(solution)/shard_map/add | solution.py:59
  50.4 0.2 reduce-scatter.2.cloned.1.call-start
  50.6 0.8 copy-done.4
  51.4 0.1 copy-done.15
  51.5 0.4 fusion.25
  51.9 0.4 fusion.27
  52.2 0.7 copy-done.3
  52.9 0.1 copy-done.13
  53.0 0.4 fusion.23
  53.3 0.7 copy-done.6
  54.1 0.4 fusion.21
  54.4 1.2 fusion.9
  55.6 1.2 fusion.8
  56.8 1.2 fusion.10
  58.1 1.2 fusion.11
  59.3 1.0 pad_maximum_fusion
  60.3 49.4 %all-reduce.2.cloned.1.call-done = f32[1024,256]{1,0:T(8,128)} async-done(((f32[1024,256]{1,0:T(8,128)}), f32[1024,256]{1,0:T(8,128)}) %all-reduce.2.cloned.1.call-update) | async-done | bytes 1048592 | tf_op jit(solution)/shard_map/psum | solution.py:65
  109.7 2.3 %copy.38 = f32[1024,256]{1,0:T(8,128)} copy(f32[1024,256]{1,0:T(8,128)} %all-reduce.2.cloned.1.call-done) | data formatting | bytes 2097152
  (46 shorter events, 0.4 us)
Async XLA Ops:
  8.0 15.3 %copy-start = (bf16[1024,256]{1,0:T(8,128)(2,1)S(1)}, bf16[1024,256]{1,0:T(8,128)(2,1)}, u32[]{:S(2)}) copy-start(bf16[1024,256]{1,0:T(8,128)(2,1)} %param.10) | copy-start | bytes 1572868
  8.0 0.8 copy-start.16
  8.0 101.7 %all-reduce.2.cloned.1.call-start = ((), (), s32[]{:S(2)}) async-start(), calls=%async_computation.1 | async-start | bytes 2097152 | tf_op jit(solution)/shard_map/psum | solution.py:65
  8.8 0.7 copy-start.17
  21.4 0.7 copy-start.18
  26.5 7.7 %copy-start.2 = (bf16[8,128,256]{2,1,0:T(8,128)(2,1)}, bf16[8,128,256]{2,1,0:T(8,128)(2,1)S(1)}, u32[]{:S(2)}) copy-start(bf16[8,128,256]{2,1,0:T(8,128)(2,1)S(1)} %gather_fusion.2) | copy-start | bytes 1572868
  27.8 2.0 %copy-start.5 = (bf16[8,128,256]{2,1,0:T(8,128)(2,1)}, bf16[8,128,256]{2,1,0:T(8,128)(2,1)S(1)}, u32[]{:S(2)}) copy-start(bf16[8,128,256]{2,1,0:T(8,128)(2,1)S(1)} %gather_fusion) | copy-start | bytes 1572868
  31.4 1.5 %copy-start.10 = (bf16[8,128,128]{2,1,0:T(8,128)(2,1)}, bf16[8,128,128]{2,1,0:T(8,128)(2,1)S(1)}, u32[]{:S(2)}) copy-start(bf16[8,128,128]{2,1,0:T(8,128)(2,1)S(1)} %fusion.4) | copy-start | bytes 786436
  34.3 1.6 %copy-start.8 = (bf16[8,128,256]{2,1,0:T(8,128)(2,1)S(1)}, bf16[8,128,256]{2,1,0:T(8,128)(2,1)}, u32[]{:S(2)}) copy-start(bf16[8,128,256]{2,1,0:T(8,128)(2,1)} %gather_fusion.3) | copy-start | bytes 1572868
  35.8 0.7 copy-start.12
  37.9 1.7 %copy-start.9 = (bf16[8,128,256]{2,1,0:T(8,128)(2,1)S(1)}, bf16[8,128,256]{2,1,0:T(8,128)(2,1)}, u32[]{:S(2)}) copy-start(bf16[8,128,256]{2,1,0:T(8,128)(2,1)} %gather_fusion.5) | copy-start | bytes 1572868
  39.6 1.4 %copy-start.14 = (bf16[8,128,128]{2,1,0:T(8,128)(2,1)}, bf16[8,128,128]{2,1,0:T(8,128)(2,1)S(1)}, u32[]{:S(2)}) copy-start(bf16[8,128,128]{2,1,0:T(8,128)(2,1)S(1)} %fusion.6) | copy-start | bytes 786436
  42.4 1.6 %copy-start.7 = (bf16[8,128,256]{2,1,0:T(8,128)(2,1)S(1)}, bf16[8,128,256]{2,1,0:T(8,128)(2,1)}, u32[]{:S(2)}) copy-start(bf16[8,128,256]{2,1,0:T(8,128)(2,1)} %gather_fusion.7) | copy-start | bytes 1572868
  45.5 1.2 %copy-start.1 = (f32[8,128,256]{2,1,0:T(8,128)S(1)}, f32[8,128,256]{2,1,0:T(8,128)}, u32[]{:S(2)}) copy-start(f32[8,128,256]{2,1,0:T(8,128)} %fusion.26) | copy-start | bytes 3145732
  50.4 1.0 copy-start.4
  50.4 1.1 copy-start.15
  50.4 59.3 %reduce-scatter.2.cloned.1.call-start = ((), (), s32[]{:S(2)}) async-start(), calls=%async_computation.2 | async-start | bytes 1310720 | tf_op jit(solution)/shard_map/reduce_scatter | solution.py:62
  51.9 1.0 copy-start.3
  51.9 1.1 copy-start.13
  53.0 1.0 copy-start.6
  53.0 1.1 copy-start.11
Sparse Core Ops, SparseCore 0:
  50.5 59.1 all-reduce.1
Sparse Core Ops, SparseCore 1:
  60.4 27.9 reduce-scatter.1
where the time goes:
time: 120 us; the launch traced here: 119 us
  waiting for transfers between devices  49.4 us (41%)
  matrix products  20.7 us (17%)
  local copies, waits for them, and re-layouts  16.9 us (14%)
  between operations  15.9 us (13%)
  blocking collectives  11.8 us (10%)
  other arithmetic  4.39 us (4%)
    psum x1, waiting for transfers between devices, body(): user_grad = lax.psum(user_total, 'strata')  49.4 us
    all_gather x1, blocking collectives, body(): gathered = lax.all_gather(item_factors, 'blk', axis=0, tiled=True)  11.8 us
    dot_general x4, matrix products, tile_terms(): jnp.einsum('kar,kbr->kab', picked_users, picked_items, preferred_element_...  6.31 us
    unnamed x39, local copies, waits for them, and re-layouts  6.27 us
    gather x4, local copies, waits for them, and re-layouts, tile_terms(): picked_items = jnp.take(panel_tiles, cols, axis=0)  5.5 us
    dot_general x4, matrix products, tile_terms(): jnp.einsum('ku,kar->uar', user_hot, user_part, precision=lax.Precision.HI...  4.7 us
    dot_general x4, matrix products, tile_terms(): jnp.einsum('kp,kbr->pbr', item_hot, item_part, precision=lax.Precision.HI...  4.68 us
    dot_general x4, matrix products, tile_terms(): jnp.einsum('kab,kbr->kar', residue, picked_items, preferred_element_type=...  3.57 us
  transfers between devices with their start and end apart: 2, of which 1 were waited for; matrix products, arithmetic and copies ran while one was open for 6% of the time, Pallas kernels for 0%

commit v1 on v0

--- a/solution.py
+++ b/solution.py
@@ -45,7 +45,26 @@
     count_sets = tile_count[0, :, 0]
     user_total = jnp.zeros(user_tiles.shape, jnp.float32)
     early = None
-    gathered = lax.all_gather(item_factors, "blk", axis=0, tiled=True)
+    size, index, width = (lax.axis_size("blk"), lax.axis_index("blk"), item_factors.shape[0])
+    forward = [(i, (i + 1) % size) for i in range(size)]
+    behind = [(i, (i - 1) % size) for i in range(size)]
+    result = jnp.zeros(
+        (*item_factors.shape[:0], size * width, *item_factors.shape[0 + 1 :]), item_factors.dtype
+    )
+    result = lax.dynamic_update_slice_in_dim(result, item_factors, index * width, axis=0)
+    from_left = from_right = item_factors
+    half = size // 2
+    for lap in range(1, half + 1):
+        from_left = lax.ppermute(from_left, "blk", forward)
+        result = lax.dynamic_update_slice_in_dim(
+            result, from_left, (index - lap) % size * width, axis=0
+        )
+        if lap < size - half:
+            from_right = lax.ppermute(from_right, "blk", behind)
+            result = lax.dynamic_update_slice_in_dim(
+                result, from_right, (index + lap) % size * width, axis=0
+            )
+    gathered = result
     pieces = []
     for source in range(steps):
         panel = gathered[source * panel_rows : (source + 1) * panel_rows]

time: 120 us -> 130 us (1.083)
  blocking collectives: 11.8 us -> 0 us
  local copies, waits for them, and re-layouts: 16.9 us -> 22.7 us
  waiting for transfers between devices: 49.4 us -> 55 us
  starting transfers between devices: 0.26 us -> 5.28 us
  matrix products: 20.7 us -> 24.4 us
  other arithmetic: 4.39 us -> 5.9 us
    all_gather x1 -> x0, blocking collectives: 11.8 us -> none  [body(): gathered = lax.all_gather(item_factors, 'blk', axis=0, tiled=True)]
    unnamed x39 -> x67, local copies, waits for them, and re-layouts: 6.27 us -> 11.7 us
    ppermute x0 -> x3, starting transfers between devices: none -> 5.02 us  [the longest x2 3.99 us: body(): from_left = lax.ppermute(from_left, 'blk', forward)]
    ppermute x0 -> x3, waiting for transfers between devices: none -> 4.82 us  [the longest x2 4.82 us: body(): from_left = lax.ppermute(from_left, 'blk', forward)]
    dot_general x4, matrix products: 1.42 us -> 5.07 us  [tile_terms(): jnp.einsum('kab,kar->kbr', residue, picked_users, preferred_element_type=...]
    gather x4, local copies, waits for them, and re-layouts: 5.5 us -> 3.11 us  [tile_terms(): picked_items = jnp.take(panel_tiles, cols, axis=0)]
    convert_element_type x4, other arithmetic: 2.57 us -> 4.22 us  [tile_terms(): live = (jnp.arange(slots) < count).astype(jnp.float32)]
    squeeze x1, local copies, waits for them, and re-layouts: 0.01 us -> 1.32 us  [body(): cols = lax.dynamic_index_in_dim(col_sets, source, 0, keepdims=False)]
  transfers between devices with their start and end apart: 2 -> 5, of which waited for: 1 -> 2; matrix products, arithmetic and copies ran while one was open for 6% -> 13% of each run, Pallas kernels for 0% -> 0%
where the time goes in v1:
time: 130 us; the launch traced here: 129 us
  waiting for transfers between devices  55 us (42%)
  matrix products  24.4 us (19%)
  local copies, waits for them, and re-layouts  22.7 us (17%)
  between operations  16 us (12%)
  other arithmetic  5.9 us (5%)
  starting transfers between devices  5.28 us (4%)
    psum x1, waiting for transfers between devices, body(): user_grad = lax.psum(user_total, 'strata')  50.2 us
    unnamed x67, local copies, waits for them, and re-layouts  11.7 us
    dot_general x4, matrix products, tile_terms(): jnp.einsum('kar,kbr->kab', picked_users, picked_items, preferred_element_...  5.5 us
    dot_general x4, matrix products, tile_terms(): jnp.einsum('kab,kar->kbr', residue, picked_users, preferred_element_type=...  5.07 us
    ppermute x2, waiting for transfers between devices, body(): from_left = lax.ppermute(from_left, 'blk', forward)  4.82 us
    dot_general x4, matrix products, tile_terms(): jnp.einsum('ku,kar->uar', user_hot, user_part, precision=lax.Precision.HI...  4.69 us
    dot_general x4, matrix products, tile_terms(): jnp.einsum('kp,kbr->pbr', item_hot, item_part, precision=lax.Precision.HI...  4.67 us
    dot_general x4, matrix products, tile_terms(): jnp.einsum('kab,kbr->kar', residue, picked_items, preferred_element_type=...  4.46 us
  transfers between devices with their start and end apart: 5, of which 2 were waited for; matrix products, arithmetic and copies ran while one was open for 13% of the time, Pallas kernels for 0%

profile of v1, /device:TPU:0, one launch (start us, length us, event | category | flops | bytes accessed | tf_op | source)
XLA Modules:
  0.0 129.3 jit_solution(7522659022180584328)
XLA Ops:
  8.1 3.0 %collective-permute-start = (bf16[256,256]{1,0:T(8,128)(2,1)}, bf16[256,256]{1,0:T(8,128)(2,1)S(1)}, u32[]{:S(2)}, u32[]{:S(2)}) collective-permute-start(bf16[256,256]{1,0:T(8,128)(2,1)} %param.11), channel_id=1, source_target_pairs={{0,8},{8,16},{16,24},{24,0},{1,9},{9,17},{17,25},{25,1},{2,10},{10... | collective-permute-start | bytes 393224 | tf_op jit(solution)/shard_map/ppermute | solution.py:58
  11.0 1.0 collective-permute-start.1
  12.1 1.3 %slice_bitcast_fusion.6 = (s32[8]{0:T(128)S(1)}, s32[8]{0:T(128)}, s32[8]{0:T(128)}, s32[8]{0:T(128)}) fusion(s32[1,4,1,8]{3,2,1,0:T(1,128)} %param.14), kind=kLoop, calls=%fused_computation.127 | loop fusion | bytes 256 | tf_op jit(solution)/shard_map/jit(dynamic_index_in_dim)/squeeze | solution.py:73
  13.4 0.6 compare_and_fusion
  14.6 0.6 copy-done.11
  15.2 0.7 fusion.78
  15.9 1.2 compare_convert_fusion.2
  17.1 0.7 compare_convert_fusion.1
  17.9 0.9 copy-done.10
  18.7 1.2 compare_convert_fusion
  19.9 1.2 compare_convert_fusion.3
  21.1 1.4 %gather_fusion.2 = bf16[8,128,256]{2,1,0:T(8,128)(2,1)} fusion(bf16[8,128,256]{2,1,0:T(8,128)(2,1)S(1)} %bitcast.99, s32[1024]{0:T(1024)S(1)} %pad_clamp_fusion.5), kind=kCustom, calls=%fused_computation.2.clone | custom fusion | bytes 1048608 | tf_op jit(solution)/shard_map/jit(_take)/gather | solution.py:10
  23.7 1.4 %gather_fusion = bf16[8,128,256]{2,1,0:T(8,128)(2,1)} fusion(bf16[8,128,256]{2,1,0:T(8,128)(2,1)S(1)} %bitcast.98, s32[1024]{0:T(1024)S(1)} %pad_clamp_fusion.7), kind=kCustom, calls=%fused_computation.clone | custom fusion | bytes 1048608 | tf_op jit(solution)/shard_map/jit(_take)/gather | solution.py:10
  25.0 1.0 collective-permute-start.2
  26.1 4.8 %collective-permute-done.2 = bf16[256,256]{1,0:T(8,128)(2,1)S(1)} collective-permute-done((bf16[256,256]{1,0:T(8,128)(2,1)S(1)}, bf16[256,256]{1,0:T(8,128)(2,1)S(1)}, u32[]{:S(2)}, u32[]{:S(2)}) %collective-permute-start.2) | collective-permute-done | bytes 131104 | tf_op jit(solution)/shard_map/ppermute | solution.py:58
  31.0 0.6 gather_fusion.5
  31.6 1.3 %fusion.6 = bf16[8,128,128]{2,1,0:T(8,128)(2,1)S(1)} fusion(f32[8]{0:T(128)S(1)} %compare_convert_fusion.1, bf16[1,4,1,8,128,128]{5,4,3,2,1,0:T(8,128)(2,1)} %param.12, bf16[8,128,256]{2,1,0:T(8,128)(2,1)S(1)} %gather_fusion.4, pred[8]{0:T(512)(128)(4,1)S(1)} %get-tuple-element.52, bf16[8,128,256]{2,1,0:T(8,128)(2,1)S(1)} %gather_fusion.5, ...), kind=kOutput, calls=%fused_computation.21 | convolution fusion | flops 68157440 | bytes 1572912 | tf_op jit(solution)/shard_map/kar,kbr->kab/dot_general | solution.py:12
  32.9 1.0 fusion.25
  34.0 1.4 %fusion.26 = f32[8,128,256]{2,1,0:T(8,128)} fusion(bf16[8,128,128]{2,1,0:T(8,128)(2,1)S(1)} %fusion.6, bf16[8,128,256]{2,1,0:T(8,128)(2,1)S(1)} %gather_fusion.5, pred[8]{0:T(512)(128)(4,1)S(1)} %copy-done.25), kind=kOutput, calls=%fused_computation.58 | convolution fusion | flops 67371008 | bytes 1835016 | tf_op jit(solution)/shard_map/kab,kbr->kar/dot_general | solution.py:20
  36.6 1.3 %fusion.5 = bf16[8,128,128]{2,1,0:T(8,128)(2,1)S(1)} fusion(f32[8]{0:T(128)S(1)} %copy-done.31, bf16[1,4,1,8,128,128]{5,4,3,2,1,0:T(8,128)(2,1)} %param.12, bf16[8,128,256]{2,1,0:T(8,128)(2,1)S(1)} %copy-done.7, pred[8]{0:T(512)(128)(4,1)S(1)} %copy-done.23, bf16[8,128,256]{2,1,0:T(8,128)(2,1)S(1)} %gather_fusion.3, pred[8]{0:T(512)(128)(4,1)S(1)} %copy-done.22), kind=kOutput, calls=%fused_computation.20 | convolution fusion | flops 68157440 | bytes 1572912 | tf_op jit(solution)/shard_map/kar,kbr->kab/dot_general | solution.py:12
  38.0 1.3 %fusion.23 = f32[8,128,256]{2,1,0:T(8,128)} fusion(bf16[8,128,128]{2,1,0:T(8,128)(2,1)S(1)} %fusion.5, bf16[8,128,256]{2,1,0:T(8,128)(2,1)S(1)} %copy-done.7, pred[8]{0:T(512)(128)(4,1)S(1)} %copy-done.23), kind=kOutput, calls=%fused_computation.55 | convolution fusion | flops 67371008 | bytes 1835016 | tf_op jit(solution)/shard_map/kab,kar->kbr/dot_general | solution.py:23
  39.3 1.3 %fusion.24 = f32[8,128,256]{2,1,0:T(8,128)} fusion(bf16[8,128,128]{2,1,0:T(8,128)(2,1)S(1)} %fusion.5, bf16[8,128,256]{2,1,0:T(8,128)(2,1)S(1)} %gather_fusion.3, pred[8]{0:T(512)(128)(4,1)S(1)} %copy-done.22), kind=kOutput, calls=%fused_computation.56 | convolution fusion | flops 67371008 | bytes 1835016 | tf_op jit(solution)/shard_map/kab,kbr->kar/dot_general | solution.py:20
  42.0 1.3 %fusion.4 = bf16[8,128,128]{2,1,0:T(8,128)(2,1)S(1)} fusion(f32[8]{0:T(128)S(1)} %copy-done.32, bf16[1,4,1,8,128,128]{5,4,3,2,1,0:T(8,128)(2,1)} %param.12, bf16[8,128,256]{2,1,0:T(8,128)(2,1)S(1)} %copy-done.6, pred[8]{0:T(512)(128)(4,1)S(1)} %copy-done.21, bf16[8,128,256]{2,1,0:T(8,128)(2,1)S(1)} %gather_fusion.1, pred[8]{0:T(512)(128)(4,1)S(1)} %copy-done.20), kind=kOutput, calls=%fused_computation.19 | convolution fusion | flops 68157440 | bytes 1572912 | tf_op jit(solution)/shard_map/kar,kbr->kab/dot_general | solution.py:12
  43.3 1.4 %fusion.21 = f32[8,128,256]{2,1,0:T(8,128)} fusion(bf16[8,128,128]{2,1,0:T(8,128)(2,1)S(1)} %fusion.4, bf16[8,128,256]{2,1,0:T(8,128)(2,1)S(1)} %copy-done.6, pred[8]{0:T(512)(128)(4,1)S(1)} %copy-done.21), kind=kOutput, calls=%fused_computation.53 | convolution fusion | flops 67371008 | bytes 1835016 | tf_op jit(solution)/shard_map/kab,kar->kbr/dot_general | solution.py:23
  44.7 1.4 %fusion.22 = f32[8,128,256]{2,1,0:T(8,128)S(1)} fusion(bf16[8,128,128]{2,1,0:T(8,128)(2,1)S(1)} %fusion.4, bf16[8,128,256]{2,1,0:T(8,128)(2,1)} %copy-done.9, pred[8]{0:T(512)(128)(4,1)S(1)} %copy-done.20), kind=kOutput, calls=%fused_computation.54 | convolution fusion | flops 67371008 | bytes 1835016 | tf_op jit(solution)/shard_map/kab,kbr->kar/dot_general | solution.py:20
  46.1 1.4 %gather_fusion.7 = bf16[8,128,256]{2,1,0:T(8,128)(2,1)} fusion(bf16[2,128,256]{2,1,0:T(8,128)(2,1)S(1)} %bitcast.103, s32[1024]{0:T(1024)S(1)} %pad_clamp_fusion), kind=kCustom, calls=%fused_computation.7.clone | custom fusion | bytes 1048608 | tf_op jit(solution)/shard_map/jit(_take)/gather | solution.py:11
  47.5 0.6 copy-done.18
  48.2 1.5 %fusion.7 = bf16[8,128,128]{2,1,0:T(8,128)(2,1)S(1)} fusion(f32[8]{0:T(128)S(1)} %copy-done.30, bf16[1,4,1,8,128,128]{5,4,3,2,1,0:T(8,128)(2,1)} %param.12, bf16[8,128,256]{2,1,0:T(8,128)(2,1)S(1)} %gather_fusion.6, pred[8]{0:T(512)(128)(4,1)S(1)} %copy-done.19, bf16[8,128,256]{2,1,0:T(8,128)(2,1)} %gather_fusion.7, pred[8]{0:T(512)(128)(4,1)S(1)} %copy-done.18), kind=kOutput, calls=%fused_computation.22 | convolution fusion | flops 68157440 | bytes 1572912 | tf_op jit(solution)/shard_map/kar,kbr->kab/dot_general | solution.py:12
  49.7 1.4 %fusion.27 = f32[8,128,256]{2,1,0:T(8,128)} fusion(bf16[8,128,128]{2,1,0:T(8,128)(2,1)S(1)} %fusion.7, bf16[8,128,256]{2,1,0:T(8,128)(2,1)S(1)} %gather_fusion.6, pred[8]{0:T(512)(128)(4,1)S(1)} %copy-done.19), kind=kOutput, calls=%fused_computation.59 | convolution fusion | flops 67371008 | bytes 1835016 | tf_op jit(solution)/shard_map/kab,kar->kbr/dot_general | solution.py:23
  52.0 1.2 fusion.12
  53.2 0.6 copy-done.29
  53.8 1.2 convolution_add_fusion.2
  55.0 0.6 copy-done.28
  55.6 1.2 convolution_add_fusion.1
  56.8 0.6 copy-done.27
  57.4 1.2 convolution_add_fusion
  58.6 1.3 copy.8
  60.1 1.0 copy-done.2
  61.1 1.2 fusion.10
  62.3 0.7 copy-done.15
  63.0 1.2 fusion.9
  64.1 0.6 copy-done.14
  64.7 1.2 fusion.8
  66.0 1.1 copy-done.1
  67.1 1.2 fusion.11
  68.4 1.0 pad_maximum_fusion
  69.4 50.2 %all-reduce.2.cloned.1.call-done = f32[1024,256]{1,0:T(8,128)} async-done(((f32[1024,256]{1,0:T(8,128)}), f32[1024,256]{1,0:T(8,128)}) %all-reduce.2.cloned.1.call-update) | async-done | bytes 1048592 | tf_op jit(solution)/shard_map/psum | solution.py:84
  119.6 2.3 %copy.42 = f32[1024,256]{1,0:T(8,128)} copy(f32[1024,256]{1,0:T(8,128)} %all-reduce.2.cloned.1.call-done) | data formatting | bytes 2097152
  (87 shorter events, 6.0 us)
Async XLA Ops:
  8.0 13.1 %copy-start = (bf16[1024,256]{1,0:T(8,128)(2,1)S(1)}, bf16[1024,256]{1,0:T(8,128)(2,1)}, u32[]{:S(2)}) copy-start(bf16[1024,256]{1,0:T(8,128)(2,1)} %param.10) | copy-start | bytes 1572868
  8.0 111.6 %all-reduce.2.cloned.1.call-start = ((), (), s32[]{:S(2)}) async-start(), calls=%async_computation.1 | async-start | bytes 2097152 | tf_op jit(solution)/shard_map/psum | solution.py:84
  8.1 17.0 %collective-permute-start = (bf16[256,256]{1,0:T(8,128)(2,1)}, bf16[256,256]{1,0:T(8,128)(2,1)S(1)}, u32[]{:S(2)}, u32[]{:S(2)}) collective-permute-start(bf16[256,256]{1,0:T(8,128)(2,1)} %param.11), channel_id=1, source_target_pairs={{0,8},{8,16},{16,24},{24,0},{1,9},{9,17},{17,25},{25,1},{2,10},{10... | collective-permute-start | bytes 393224 | tf_op jit(solution)/shard_map/ppermute | solution.py:58
  11.0 15.0 %collective-permute-start.1 = (bf16[256,256]{1,0:T(8,128)(2,1)}, bf16[256,256]{1,0:T(8,128)(2,1)S(1)}, u32[]{:S(2)}, u32[]{:S(2)}) collective-permute-start(bf16[256,256]{1,0:T(8,128)(2,1)} %param.11), channel_id=1, source_target_pairs={{0,24},{8,0},{16,8},{24,16},{1,25},{9,1},{17,9},{25,17},{2,26},{10... | collective-permute-start | bytes 393224 | tf_op jit(solution)/shard_map/ppermute | solution.py:63
  12.1 1.3 %copy-start.12 = (s32[1,4,1,8]{3,2,1,0:T(1,128)S(1)}, s32[1,4,1,8]{3,2,1,0:T(1,128)}, u32[]{:S(2)}) copy-start(s32[1,4,1,8]{3,2,1,0:T(1,128)} %param.14) | copy-start | bytes 388
  12.1 1.3 %copy-start.13 = (s32[1,4,1,8]{3,2,1,0:T(1,128)S(1)}, s32[1,4,1,8]{3,2,1,0:T(1,128)}, u32[]{:S(2)}) copy-start(s32[1,4,1,8]{3,2,1,0:T(1,128)} %param.13) | copy-start | bytes 388
  14.0 17.6 %copy-start.24 = (pred[8]{0:T(512)(128)(4,1)}, pred[8]{0:T(512)(128)(4,1)S(1)}, u32[]{:S(2)}) copy-start(pred[8]{0:T(512)(128)(4,1)S(1)} %get-tuple-element.32) | copy-start | bytes 28
  14.0 17.6 %copy-start.26 = (pred[8]{0:T(512)(128)(4,1)}, pred[8]{0:T(512)(128)(4,1)S(1)}, u32[]{:S(2)}) copy-start(pred[8]{0:T(512)(128)(4,1)S(1)} %get-tuple-element.52) | copy-start | bytes 28
  14.6 0.7 copy-start.11
  17.8 0.9 copy-start.10
  25.0 5.9 %collective-permute-start.2 = (bf16[256,256]{1,0:T(8,128)(2,1)S(1)}, bf16[256,256]{1,0:T(8,128)(2,1)S(1)}, u32[]{:S(2)}, u32[]{:S(2)}) collective-permute-start(bf16[256,256]{1,0:T(8,128)(2,1)S(1)} %collective-permute-done), channel_id=1, source_target_pairs={{0,8},{8,16},{16,24},{24,0},{1,9},{9,17},{17,25},{25,1},{2,10},{10... | collective-permute-start | bytes 393224 | tf_op jit(solution)/shard_map/ppermute | solution.py:58
  32.9 1.0 copy-start.25
  35.3 1.0 copy-start.7
  35.9 0.7 copy-start.22
  35.9 0.7 copy-start.23
  35.9 0.7 copy-start.31
  40.6 1.0 copy-start.6
  41.2 2.1 %copy-start.9 = (bf16[8,128,256]{2,1,0:T(8,128)(2,1)}, bf16[8,128,256]{2,1,0:T(8,128)(2,1)S(1)}, u32[]{:S(2)}) copy-start(bf16[8,128,256]{2,1,0:T(8,128)(2,1)S(1)} %gather_fusion.1) | copy-start | bytes 1572868
  41.2 0.7 copy-start.20
  41.2 0.7 copy-start.21
  41.2 0.7 copy-start.32
  47.5 0.6 copy-start.18
  47.5 0.7 copy-start.19
  47.5 0.7 copy-start.30
  49.6 1.4 %copy-start.8 = (bf16[8,128,256]{2,1,0:T(8,128)(2,1)S(1)}, bf16[8,128,256]{2,1,0:T(8,128)(2,1)}, u32[]{:S(2)}) copy-start(bf16[8,128,256]{2,1,0:T(8,128)(2,1)} %gather_fusion.7) | copy-start | bytes 1572868
  51.4 0.6 copy-start.17
  52.0 1.2 copy-start.5
  53.2 0.6 copy-start.29
  53.8 1.2 copy-start.3
  55.0 0.6 copy-start.28
  56.8 0.6 copy-start.27
  59.9 1.2 copy-start.2
  59.9 1.2 copy-start.16
  59.9 59.7 %reduce-scatter.2.cloned.1.call-start = ((), (), s32[]{:S(2)}) async-start(), calls=%async_computation.2 | async-start | bytes 1310720 | tf_op jit(solution)/shard_map/reduce_scatter | solution.py:81
  61.1 3.0 %copy-start.4 = (f32[8,128,256]{2,1,0:T(8,128)S(1)}, f32[8,128,256]{2,1,0:T(8,128)}, u32[]{:S(2)}) copy-start(f32[8,128,256]{2,1,0:T(8,128)} %fusion.27) | copy-start | bytes 3145732
  62.3 0.7 copy-start.15
  64.1 0.6 copy-start.14
  65.9 1.2 copy-start.1
Sparse Core Ops, SparseCore 0:
  60.0 59.5 all-reduce.1
Sparse Core Ops, SparseCore 1:
  69.5 28.4 reduce-scatter.1
